TPU v7x, 128 devices: a whole 4x4x4 slice. The times are simulated.
128 devices in a mesh: orient: 32 (over x, z, y_lo), slab: 4 (over y_hi, core).
Axes of the slice: x: 4, y: 4 (y_hi: 2, y_lo: 2; y = y_hi * 2 + y_lo), z: 4, core: 2. Of those that a mesh axis runs over, the one named last changes fastest.
Arguments:
- volume: bfloat16 [32, 512, 8192], P('orient', 'slab'), may hold values from 0 to 2
- rays: bfloat16 [8192, 8, 128], replicated, may hold values from -0.0234375 to 0.0234375
- band_start: int32 [8, 32], P(None, 'orient'), may hold values from 0 to 63
- band_len: int32 [8, 32], P(None, 'orient'), may hold values from 32 to 64
- slot_image: int32 [32], replicated, may hold values from 0 to 31, each once
- measured: float32 [32, 512, 128], P('orient', 'slab'), may hold values from -6 to 6
- relax: float32 [32], P('orient'), may hold values from 0.25 to 1
Outputs:
- updated: bfloat16 [32, 512, 8192], P('orient', 'slab')
- residual: float32 [32, 512, 128], P('orient', 'slab')
Inputs may be any that keep to these rules, and one draw needn't show every extreme that they name: `slot_image`: every image number appears in exactly one slot. band_start + band_len stays below 128.
All inputs are finite; a program needn't handle non-finite values.
Results may differ from a plain program's by a relative error of at most 0.0055.
Values may be sent and summed in bfloat16 or wider, within the bound.
No kernel may reach another device: no remote copies, remote signals or barrier semaphores. Data moves between devices by JAX's collectives and lax.ppermute only.
A program may use at most 128 MiB of HBM per device.

v0:
```python
import math
import jax
import jax.numpy as jnp
from jax import lax
from jax.sharding import PartitionSpec as P

FRAMES = 4
SWEEPS = 2
huber_delta = 0.5
sweep_rate = 0.2


def extended_2(cells, sides, width):
    for axis, dim in sides:
        count = lax.axis_size(axis)
        ends = count - 1
        head = lax.slice_in_dim(cells, 0, width, axis=dim)
        tail = lax.slice_in_dim(cells, cells.shape[dim] - width, cells.shape[dim], axis=dim)
        cells = jnp.concatenate(
            [
                lax.ppermute(tail, axis, [(i, (i + 1) % count) for i in range(ends)]),
                cells,
                lax.ppermute(head, axis, [((i + 1) % count, i) for i in range(ends)]),
            ],
            axis=dim,
        )
    return cells


def smooth_pass(extended, first_row, total_rows):
    middle = extended[:, 1:-1]
    row_count = middle.shape[1]
    global_rows = first_row + 1 + jnp.arange(row_count, dtype=jnp.int32)
    has_above = (global_rows > 0)[None, :, None]
    has_below = (global_rows < total_rows - 1)[None, :, None]
    from_above = jnp.clip(middle - extended[:, :-2], -huber_delta, huber_delta)
    from_below = jnp.clip(middle - extended[:, 2:], -huber_delta, huber_delta)
    row_flux = jnp.where(has_above, from_above, 0.0) + jnp.where(has_below, from_below, 0.0)
    return middle - sweep_rate * row_flux


def local(volume, rays, band_start, band_len, slot_image, measured, relax):
    or_dev, row_dev, cell_count = volume.shape
    reflections_n, detector = (rays.shape[1], rays.shape[2])
    images_n = reflections_n * FRAMES
    orient_groups = lax.axis_size("orient")
    orients_all = or_dev * orient_groups
    orient_ids = lax.axis_index("orient") * or_dev + jnp.arange(or_dev, dtype=jnp.int32)
    reflections = jnp.arange(reflections_n, dtype=jnp.int32)
    frame_of = (orient_ids[:, None] + reflections[None, :]) % FRAMES
    frame_pick = (frame_of[:, :, None] == jnp.arange(FRAMES, dtype=jnp.int32)).astype(jnp.float32)
    columns = jnp.arange(detector, dtype=jnp.int32)
    inside = (columns >= band_start[:, :, None]) & (columns < (band_start + band_len)[:, :, None])
    band_mask = inside.astype(jnp.float32)
    inverse = (
        jnp.zeros((images_n,), jnp.int32).at[slot_image].set(jnp.arange(images_n, dtype=jnp.int32))
    )
    flat_rays = rays.reshape(cell_count, reflections_n * detector)
    projected = jnp.dot(
        volume.reshape(or_dev * row_dev, cell_count), flat_rays, preferred_element_type=jnp.float32
    )
    projected = projected.reshape(or_dev, row_dev, reflections_n, detector)
    evolved = jnp.einsum("okf,kod,orkd->kfrd", frame_pick, band_mask, projected)
    ordered = evolved.reshape(images_n, row_dev, detector)[slot_image]
    owned = lax.psum_scatter(ordered, "orient", scatter_dimension=0, tiled=True)
    residual = measured - owned
    everyone = lax.all_gather(residual.astype(jnp.bfloat16), "orient", axis=0, tiled=True)
    by_image = everyone[inverse].reshape(reflections_n, FRAMES, row_dev, detector)
    picked = by_image[reflections[None, :], frame_of]
    masked = picked * jnp.transpose(band_mask, (1, 0, 2))[:, :, None, :].astype(jnp.bfloat16)
    gradient = jnp.einsum("okrd,ckd->orc", masked, rays, preferred_element_type=jnp.float32)
    step_gain = math.sqrt(cell_count * orients_all / (FRAMES * reflections_n * detector))
    density = volume.astype(jnp.float32) + relax[:, None, None] * step_gain * gradient
    total_rows = row_dev * lax.axis_size("slab")
    base_row = lax.axis_index("slab") * row_dev
    for repeat in range(SWEEPS):
        extended = extended_2(density, (("slab", 1),), 1)
        density = smooth_pass(extended, base_row - 1, total_rows)
    return (density.astype(jnp.bfloat16), residual)


def solution(mesh):
    placed = (
        P("orient", "slab", None),
        P(),
        P(None, "orient"),
        P(None, "orient"),
        P(),
        P("orient", "slab", None),
        P("orient"),
    )
    return jax.shard_map(
        local,
        mesh=mesh,
        in_specs=placed,
        out_specs=(P("orient", "slab", None), P("orient", "slab", None)),
        check_vma=False,
    )
```

profile of v0, /device:TPU:1, one launch (start us, length us, event | category | flops | bytes accessed | tf_op | source)
XLA Modules:
  0.0 423.8 jit_solution(1588492112718736785)
XLA Ops:
  7.2 15.6 %copy.30 = bf16[1024,8,8,128]{3,1,2,0:T(8,128)(2,1)} copy(bf16[1024,8,8,128]{3,2,1,0:T(8,128)(2,1)} %bitcast.48) | data formatting | bytes 33554432
  22.8 21.1 %copy.15 = bf16[1024,8192]{1,0:T(8,128)(2,1)} copy(bf16[1024,8192]{0,1:T(8,128)(2,1)} %bitcast.47) | data formatting | bytes 33554432 | tf_op jit(solution)/shard_map/dot_general | solution.py:59
  43.9 0.1 fusion.46
  44.0 8.1 %fusion.38 = f32[8,128,128]{1,2,0:T(8,128)S(1)} fusion(bf16[8,128,8192]{2,1,0:T(8,128)(2,1)} %bitcast.49, bf16[1,128,8192]{2,1,0:T(8,128)(2,1)S(1)} %copy-done.2, f32[8,128]{1,0:T(8,128)S(1)} %get-tuple-element.9), kind=kOutput, calls=%fused_computation.37 | convolution fusion | flops 2147614720 | bytes 19402752 | tf_op jit(solution)/shard_map/dot_general | solution.py:59
  52.2 0.2 copy.16
  52.4 0.1 fusion.43
  52.5 0.2 broadcast_multiply_fusion
  52.7 2.0 gather_fusion
  54.8 144.4 %reduce-scatter.2.cloned.1.call-done = f32[1,128,128]{2,1,0:T(8,128)} async-done(((f32[32,128,128]{2,1,0:T(8,128)}), f32[1,128,128]{2,1,0:T(8,128)}) %reduce-scatter.2.cloned.1.call-update) | async-done | bytes 65552 | tf_op jit(solution)/shard_map/reduce_scatter | solution.py:65
  199.1 1.5 fusion.53
  201.3 0.7 scatter_custom_fusion
  202.1 147.3 %all-gather.2.cloned.1.call-done = bf16[32,128,128]{2,1,0:T(8,128)(2,1)} async-done(((bf16[1,128,128]{2,1,0:T(8,128)(2,1)}), bf16[32,128,128]{2,1,0:T(8,128)(2,1)}) %all-gather.2.cloned.1.call-update) | async-done | bytes 1048592 | tf_op jit(solution)/shard_map/all_gather | solution.py:67
  349.3 2.0 gather_fusion.1
  351.3 0.6 gather_fusion.2
  351.9 14.0 %fusion.11 = f32[1,128,8192]{2,1,0:T(8,128)} fusion(bf16[8192,8,128]{2,1,0:T(8,128)(2,1)} %param.8, bf16[1,128,8192]{2,1,0:T(8,128)(2,1)} %param.7, f32[]{:T(128)} %bitcast, bf16[8,128,128]{2,1,0:T(8,128)(2,1)S(1)} %gather_fusion.2, bf16[8,128]{1,0:T(8,128)(2,1)S(1)} %get-tuple-element.8), kind=kOutput, calls=%fused_computation.10 | convolution fusion | flops 2150760448 | bytes 23332868 | tf_op jit(solution)/shard_map/okrd,ckd->orc/dot_general | solution.py:71
  365.9 1.1 fusion.55
  367.0 25.5 %collective-permute-start.1 = (f32[1,1,8192]{2,1,0:T(1,128)S(1)}, f32[1,1,8192]{2,1,0:T(1,128)S(1)}, u32[]{:S(2)}, u32[]{:S(2)}) collective-permute-start(f32[1,1,8192]{2,1,0:T(1,128)S(1)} %get-tuple-element.7), channel_id=1, source_target_pairs={{1,0},{2,1},{3,2},{5,4},{6,5},{7,6},{9,8},{10,9},{11,10},{13,12},{... | collective-permute-start | bytes 98312 | tf_op jit(solution)/shard_map/ppermute | solution.py:23
  392.5 4.6 %collective-permute-start = (f32[1,1,8192]{2,1,0:T(1,128)S(1)}, f32[1,1,8192]{2,1,0:T(1,128)S(1)}, u32[]{:S(2)}, u32[]{:S(2)}) collective-permute-start(f32[1,1,8192]{2,1,0:T(1,128)S(1)} %get-tuple-element.6), channel_id=1, source_target_pairs={{0,1},{1,2},{2,3},{4,5},{5,6},{6,7},{8,9},{9,10},{10,11},{12,13},{... | collective-permute-start | bytes 98312 | tf_op jit(solution)/shard_map/ppermute | solution.py:21
  397.1 1.0 collective-permute-done
  398.1 6.0 %fusion.29 = f32[1,128,8192]{2,1,0:T(8,128)S(1)} fusion(f32[1,128,8192]{2,1,0:T(8,128)} %fusion.11, f32[1,1,8192]{2,1,0:T(1,128)S(1)} %collective-permute-done.1, f32[1,1,8192]{2,1,0:T(1,128)S(1)} %collective-permute-done, pred[128]{0:T(512)(128)(4,1)S(1)} %get-tuple-element.10, pred[128]{0:T(512)(128)(4,1)S(1)} %get-tuple-element.11), kind=kLoop, calls=%fused_computation.29 | loop fusion | flops 11534336 | bytes 8454400 | tf_op jit(solution)/shard_map/sub | solution.py:39
  404.1 1.9 collective-permute-start.3
  406.1 5.7 %collective-permute-start.2 = (f32[1,1,8192]{2,1,0:T(1,128)S(1)}, f32[1,1,8192]{2,1,0:T(1,128)S(1)}, u32[]{:S(2)}, u32[]{:S(2)}) collective-permute-start(f32[1,1,8192]{2,1,0:T(1,128)S(1)} %get-tuple-element.4), channel_id=1, source_target_pairs={{0,1},{1,2},{2,3},{4,5},{5,6},{6,7},{8,9},{9,10},{10,11},{12,13},{... | collective-permute-start | bytes 98312 | tf_op jit(solution)/shard_map/ppermute | solution.py:21
  411.8 1.0 collective-permute-done.2
  412.8 4.2 fusion.20
  (29 shorter events, 0.3 us)
Async XLA Ops:
  7.2 192.0 %reduce-scatter.2.cloned.1.call-start = ((), (), s32[]{:S(2)}) async-start(), calls=%async_computation.1 | async-start | bytes 2162688 | tf_op jit(solution)/shard_map/reduce_scatter | solution.py:65
  22.8 21.1 %copy-start.1 = (s32[8,1]{0,1:T(1,128)S(1)}, s32[8,1]{0,1:T(1,128)}, u32[]{:S(2)}) copy-start(s32[8,1]{0,1:T(1,128)} %param.9) | copy-start | bytes 100
  22.8 21.1 %copy-start.3 = (s32[8,1]{0,1:T(1,128)S(1)}, s32[8,1]{0,1:T(1,128)}, u32[]{:S(2)}) copy-start(s32[8,1]{0,1:T(1,128)} %param.10) | copy-start | bytes 100
  22.8 21.2 %copy-start.2 = (bf16[1,128,8192]{2,1,0:T(8,128)(2,1)S(1)}, bf16[1,128,8192]{2,1,0:T(8,128)(2,1)}, u32[]{:S(2)}) copy-start(bf16[1,128,8192]{2,1,0:T(8,128)(2,1)} %param.7) | copy-start | bytes 6291460
  44.0 8.4 %copy-start.4 = (s32[32]{0:T(128)S(1)}, s32[32]{0:T(128)}, u32[]{:S(2)}) copy-start(s32[32]{0:T(128)} %param.11) | copy-start | bytes 388
  52.5 146.7 %copy-start = (f32[1,128,128]{2,1,0:T(8,128)S(1)}, f32[1,128,128]{2,1,0:T(8,128)}, u32[]{:S(2)}) copy-start(f32[1,128,128]{2,1,0:T(8,128)} %param.12) | copy-start | bytes 196612
  54.7 294.6 %all-gather.2.cloned.1.call-start = ((), (), s32[]{:S(2)}) async-start(), calls=%async_computation.2 | async-start | bytes 1081344 | tf_op jit(solution)/shard_map/all_gather | solution.py:67
  367.0 30.1 %collective-permute-start.1 = (f32[1,1,8192]{2,1,0:T(1,128)S(1)}, f32[1,1,8192]{2,1,0:T(1,128)S(1)}, u32[]{:S(2)}, u32[]{:S(2)}) collective-permute-start(f32[1,1,8192]{2,1,0:T(1,128)S(1)} %get-tuple-element.7), channel_id=1, source_target_pairs={{1,0},{2,1},{3,2},{5,4},{6,5},{7,6},{9,8},{10,9},{11,10},{13,12},{... | collective-permute-start | bytes 98312 | tf_op jit(solution)/shard_map/ppermute | solution.py:23
  392.5 5.6 %collective-permute-start = (f32[1,1,8192]{2,1,0:T(1,128)S(1)}, f32[1,1,8192]{2,1,0:T(1,128)S(1)}, u32[]{:S(2)}, u32[]{:S(2)}) collective-permute-start(f32[1,1,8192]{2,1,0:T(1,128)S(1)} %get-tuple-element.6), channel_id=1, source_target_pairs={{0,1},{1,2},{2,3},{4,5},{5,6},{6,7},{8,9},{9,10},{10,11},{12,13},{... | collective-permute-start | bytes 98312 | tf_op jit(solution)/shard_map/ppermute | solution.py:21
  404.1 7.7 %collective-permute-start.3 = (f32[1,1,8192]{2,1,0:T(1,128)S(1)}, f32[1,1,8192]{2,1,0:T(1,128)S(1)}, u32[]{:S(2)}, u32[]{:S(2)}) collective-permute-start(f32[1,1,8192]{2,1,0:T(1,128)S(1)} %get-tuple-element.5), channel_id=1, source_target_pairs={{1,0},{2,1},{3,2},{5,4},{6,5},{7,6},{9,8},{10,9},{11,10},{13,12},{... | collective-permute-start | bytes 98312 | tf_op jit(solution)/shard_map/ppermute | solution.py:23
  406.1 6.7 %collective-permute-start.2 = (f32[1,1,8192]{2,1,0:T(1,128)S(1)}, f32[1,1,8192]{2,1,0:T(1,128)S(1)}, u32[]{:S(2)}, u32[]{:S(2)}) collective-permute-start(f32[1,1,8192]{2,1,0:T(1,128)S(1)} %get-tuple-element.4), channel_id=1, source_target_pairs={{0,1},{1,2},{2,3},{4,5},{5,6},{6,7},{8,9},{9,10},{10,11},{12,13},{... | collective-permute-start | bytes 98312 | tf_op jit(solution)/shard_map/ppermute | solution.py:21
Sparse Core Ops, SparseCore 0:
  54.9 144.2 reduce-scatter.1
  201.3 147.9 all-gather.1
where the time goes:
time: 425 us; the launch traced here: 424 us
  waiting for transfers between devices  294 us (69%)
  local copies, waits for them, and re-layouts  43.3 us (10%)
  starting transfers between devices  37.8 us (9%)
  matrix products  22.1 us (5%)
  between operations  14.9 us (4%)
  other arithmetic  12.1 us (3%)
    all_gather x1, waiting for transfers between devices, local(): lax.all_gather(residual.astype(jnp.bfloat16), 'orient', axis=0, tiled=True)  147 us
    reduce_scatter x1, waiting for transfers between devices, local(): owned = lax.psum_scatter(ordered, 'orient', scatter_dimension=0, tiled=True)  144 us
    ppermute x2, starting transfers between devices, extended_2(): lax.ppermute(head, axis, [((i + 1) % count, i) for i in range(ends)])  27.4 us
    dot_general x1, local copies, waits for them, and re-layouts, local(): jnp.dot(volume.reshape(or_dev * row_dev, cell_count), flat_rays, preferre...  21.1 us
    unnamed x11, local copies, waits for them, and re-layouts  15.6 us
    dot_general x1, matrix products, local(): jnp.einsum('okrd,ckd->orc', masked, rays, preferred_element_type=jnp.floa...  14 us
    ppermute x2, starting transfers between devices, extended_2(): lax.ppermute(tail, axis, [(i, (i + 1) % count) for i in range(ends)])  10.3 us
  transfers between devices with their start and end apart: 6, of which 4 were waited for; matrix products, arithmetic and copies ran while one was open for 0% of the time, Pallas kernels for 0%

commit v1 on v0

--- a/solution.py
+++ b/solution.py
@@ -64,7 +64,12 @@
     ordered = evolved.reshape(images_n, row_dev, detector)[slot_image]
     owned = lax.psum_scatter(ordered, "orient", scatter_dimension=0, tiled=True)
     residual = measured - owned
-    everyone = lax.all_gather(residual.astype(jnp.bfloat16), "orient", axis=0, tiled=True)
+    everyone = jnp.concatenate(
+        lax.all_to_all(
+            jnp.stack([residual.astype(jnp.bfloat16)] * lax.axis_size("orient")), "orient", 0, 0
+        ),
+        axis=0,
+    )
     by_image = everyone[inverse].reshape(reflections_n, FRAMES, row_dev, detector)
     picked = by_image[reflections[None, :], frame_of]
     masked = picked * jnp.transpose(band_mask, (1, 0, 2))[:, :, None, :].astype(jnp.bfloat16)

time: 425 us -> 295 us (0.69)
  waiting for transfers between devices: 294 us -> 158 us
  starting transfers between devices: 37.8 us -> 43.5 us
    all_gather x1 -> x0, waiting for transfers between devices: 147 us -> none  [local(): lax.all_gather(residual.astype(jnp.bfloat16), 'orient', axis=0, tiled=True)]
    all_to_all x0 -> x1, waiting for transfers between devices: none -> 10.7 us  [local(): lax.all_to_all(jnp.stack([residual.astype(jnp.bfloat16)] * lax.axis_size(...]
where the time goes in v1:
time: 295 us; the launch traced here: 294 us
  waiting for transfers between devices  158 us (54%)
  local copies, waits for them, and re-layouts  43.7 us (15%)
  starting transfers between devices  43.5 us (15%)
  matrix products  22.1 us (7%)
  between operations  14.9 us (5%)
  other arithmetic  12.3 us (4%)
    reduce_scatter x1, waiting for transfers between devices, local(): owned = lax.psum_scatter(ordered, 'orient', scatter_dimension=0, tiled=True)  145 us
    ppermute x2, starting transfers between devices, extended_2(): lax.ppermute(head, axis, [((i + 1) % count, i) for i in range(ends)])  29.8 us
    dot_general x1, local copies, waits for them, and re-layouts, local(): jnp.dot(volume.reshape(or_dev * row_dev, cell_count), flat_rays, preferre...  21.5 us
    unnamed x11, local copies, waits for them, and re-layouts  15.6 us
    dot_general x1, matrix products, local(): jnp.einsum('okrd,ckd->orc', masked, rays, preferred_element_type=jnp.floa...  14 us
    all_to_all x1, waiting for transfers between devices, local(): lax.all_to_all(jnp.stack([residual.astype(jnp.bfloat16)] * lax.axis_size(...  10.7 us
    ppermute x2, starting transfers between devices, extended_2(): lax.ppermute(tail, axis, [(i, (i + 1) % count) for i in range(ends)])  9.73 us
    dot_general x1, matrix products, local(): jnp.dot(volume.reshape(or_dev * row_dev, cell_count), flat_rays, preferre...  8.14 us
  transfers between devices with their start and end apart: 6, of which 4 were waited for; matrix products, arithmetic and copies ran while one was open for 0% of the time, Pallas kernels for 0%

profile of v1, /device:TPU:1, one launch (start us, length us, event | category | flops | bytes accessed | tf_op | source)
XLA Modules:
  0.0 294.2 jit_solution(17373795660445218193)
XLA Ops:
  7.2 15.6 %copy.27 = bf16[1024,8,8,128]{3,1,2,0:T(8,128)(2,1)} copy(bf16[1024,8,8,128]{3,2,1,0:T(8,128)(2,1)} %bitcast.51) | data formatting | bytes 33554432
  22.8 21.5 %copy.12 = bf16[1024,8192]{1,0:T(8,128)(2,1)} copy(bf16[1024,8192]{0,1:T(8,128)(2,1)} %bitcast.50) | data formatting | bytes 33554432 | tf_op jit(solution)/shard_map/dot_general | solution.py:59
  44.4 8.1 %fusion.38 = f32[8,128,128]{1,2,0:T(8,128)S(1)} fusion(bf16[8,128,8192]{2,1,0:T(8,128)(2,1)} %bitcast.52, bf16[1,128,8192]{2,1,0:T(8,128)(2,1)S(1)} %copy-done.2, f32[8,128]{1,0:T(8,128)S(1)} %get-tuple-element.9), kind=kOutput, calls=%fused_computation.37 | convolution fusion | flops 2147614720 | bytes 19402752 | tf_op jit(solution)/shard_map/dot_general | solution.py:59
  52.5 0.2 copy.13
  52.9 0.2 broadcast_multiply_fusion
  53.1 2.0 gather_fusion
  55.1 145.1 %reduce-scatter.2.cloned.1.call-done = f32[1,128,128]{2,1,0:T(8,128)} async-done(((f32[32,128,128]{2,1,0:T(8,128)}), f32[1,128,128]{2,1,0:T(8,128)}) %reduce-scatter.2.cloned.1.call-update) | async-done | bytes 65552 | tf_op jit(solution)/shard_map/reduce_scatter | solution.py:65
  200.2 1.5 convert_bitcast_fusion
  201.7 1.2 stack.2
  202.9 3.9 %all-to-all-start = ((bf16[32,1,128,128]{3,2,1,0:T(8,128)(2,1)}), bf16[32,1,128,128]{3,2,1,0:T(8,128)(2,1)S(1)}, u32[]{:S(2)}, u32[]{:S(2)}) async-start(bf16[32,1,128,128]{3,2,1,0:T(8,128)(2,1)} %stack.2), calls=%async_computation.1 | async-start | bytes 2097152 | tf_op jit(solution)/shard_map/all_to_all | solution.py:68
  207.5 0.7 scatter_custom_fusion
  208.2 10.7 %all-to-all-done = bf16[32,1,128,128]{3,2,1,0:T(8,128)(2,1)S(1)} async-done(((bf16[32,1,128,128]{3,2,1,0:T(8,128)(2,1)}), bf16[32,1,128,128]{3,2,1,0:T(8,128)(2,1)S(1)}, u32[]{:S(2)}, u32[]{:S(2)}) %all-to-all-start) | async-done | bytes 1048608 | tf_op jit(solution)/shard_map/all_to_all | solution.py:68
  218.9 0.7 gather_fusion.1
  219.7 0.6 gather_fusion.2
  220.3 14.0 %fusion.11 = f32[1,128,8192]{2,1,0:T(8,128)} fusion(bf16[8192,8,128]{2,1,0:T(8,128)(2,1)} %param.8, bf16[1,128,8192]{2,1,0:T(8,128)(2,1)} %param.7, f32[]{:T(128)} %bitcast, bf16[8,128,128]{2,1,0:T(8,128)(2,1)S(1)} %gather_fusion.2, bf16[8,128]{1,0:T(8,128)(2,1)S(1)} %get-tuple-element.8), kind=kOutput, calls=%fused_computation.10 | convolution fusion | flops 2150760448 | bytes 23332868 | tf_op jit(solution)/shard_map/okrd,ckd->orc/dot_general | solution.py:76
  234.3 1.1 fusion.54
  235.4 27.9 %collective-permute-start.1 = (f32[1,1,8192]{2,1,0:T(1,128)S(1)}, f32[1,1,8192]{2,1,0:T(1,128)S(1)}, u32[]{:S(2)}, u32[]{:S(2)}) collective-permute-start(f32[1,1,8192]{2,1,0:T(1,128)S(1)} %get-tuple-element.7), channel_id=1, source_target_pairs={{1,0},{2,1},{3,2},{5,4},{6,5},{7,6},{9,8},{10,9},{11,10},{13,12},{... | collective-permute-start | bytes 98312 | tf_op jit(solution)/shard_map/ppermute | solution.py:23
  263.2 4.0 %collective-permute-start = (f32[1,1,8192]{2,1,0:T(1,128)S(1)}, f32[1,1,8192]{2,1,0:T(1,128)S(1)}, u32[]{:S(2)}, u32[]{:S(2)}) collective-permute-start(f32[1,1,8192]{2,1,0:T(1,128)S(1)} %get-tuple-element.6), channel_id=1, source_target_pairs={{0,1},{1,2},{2,3},{4,5},{5,6},{6,7},{8,9},{9,10},{10,11},{12,13},{... | collective-permute-start | bytes 98312 | tf_op jit(solution)/shard_map/ppermute | solution.py:21
  267.3 1.0 collective-permute-done
  268.3 6.2 %fusion.29 = f32[1,128,8192]{2,1,0:T(8,128)S(1)} fusion(f32[1,128,8192]{2,1,0:T(8,128)} %fusion.11, f32[1,1,8192]{2,1,0:T(1,128)S(1)} %collective-permute-done.1, f32[1,1,8192]{2,1,0:T(1,128)S(1)} %collective-permute-done, pred[128]{0:T(512)(128)(4,1)S(1)} %get-tuple-element.10, pred[128]{0:T(512)(128)(4,1)S(1)} %get-tuple-element.11), kind=kLoop, calls=%fused_computation.29 | loop fusion | flops 11534336 | bytes 8454400 | tf_op jit(solution)/shard_map/sub | solution.py:39
  274.5 1.9 collective-permute-start.3
  276.5 5.7 %collective-permute-start.2 = (f32[1,1,8192]{2,1,0:T(1,128)S(1)}, f32[1,1,8192]{2,1,0:T(1,128)S(1)}, u32[]{:S(2)}, u32[]{:S(2)}) collective-permute-start(f32[1,1,8192]{2,1,0:T(1,128)S(1)} %get-tuple-element.4), channel_id=1, source_target_pairs={{0,1},{1,2},{2,3},{4,5},{5,6},{6,7},{8,9},{9,10},{10,11},{12,13},{... | collective-permute-start | bytes 98312 | tf_op jit(solution)/shard_map/ppermute | solution.py:21
  282.2 1.0 collective-permute-done.2
  283.2 4.2 %fusion.20 = bf16[1,128,8192]{2,1,0:T(8,128)(2,1)} fusion(f32[1,128,8192]{2,1,0:T(8,128)S(1)} %fusion.29, f32[1,1,8192]{2,1,0:T(1,128)S(1)} %collective-permute-done.3, f32[1,1,8192]{2,1,0:T(1,128)S(1)} %collective-permute-done.2, pred[128]{0:T(512)(128)(4,1)S(1)} %get-tuple-element.10, pred[128]{0:T(512)(128)(4,1)S(1)} %get-tuple-element.11), kind=kLoop, calls=%fused_computation.18 | loop fusion | flops 12582912 | bytes 6357248 | tf_op jit(solution)/shard_map/convert_element_type | solution.py:84
  (29 shorter events, 0.4 us)
Async XLA Ops:
  7.2 193.0 %reduce-scatter.2.cloned.1.call-start = ((), (), s32[]{:S(2)}) async-start(), calls=%async_computation.2 | async-start | bytes 2162688 | tf_op jit(solution)/shard_map/reduce_scatter | solution.py:65
  22.8 21.5 %copy-start.1 = (s32[8,1]{0,1:T(1,128)S(1)}, s32[8,1]{0,1:T(1,128)}, u32[]{:S(2)}) copy-start(s32[8,1]{0,1:T(1,128)} %param.9) | copy-start | bytes 100
  22.8 21.5 %copy-start.3 = (s32[8,1]{0,1:T(1,128)S(1)}, s32[8,1]{0,1:T(1,128)}, u32[]{:S(2)}) copy-start(s32[8,1]{0,1:T(1,128)} %param.10) | copy-start | bytes 100
  22.8 21.6 %copy-start.2 = (bf16[1,128,8192]{2,1,0:T(8,128)(2,1)S(1)}, bf16[1,128,8192]{2,1,0:T(8,128)(2,1)}, u32[]{:S(2)}) copy-start(bf16[1,128,8192]{2,1,0:T(8,128)(2,1)} %param.7) | copy-start | bytes 6291460
  44.4 8.4 %copy-start.4 = (s32[32]{0:T(128)S(1)}, s32[32]{0:T(128)}, u32[]{:S(2)}) copy-start(s32[32]{0:T(128)} %param.11) | copy-start | bytes 388
  52.8 147.3 %copy-start = (f32[1,128,128]{2,1,0:T(8,128)S(1)}, f32[1,128,128]{2,1,0:T(8,128)}, u32[]{:S(2)}) copy-start(f32[1,128,128]{2,1,0:T(8,128)} %param.12) | copy-start | bytes 196612
  202.9 16.1 %all-to-all-start = ((bf16[32,1,128,128]{3,2,1,0:T(8,128)(2,1)}), bf16[32,1,128,128]{3,2,1,0:T(8,128)(2,1)S(1)}, u32[]{:S(2)}, u32[]{:S(2)}) async-start(bf16[32,1,128,128]{3,2,1,0:T(8,128)(2,1)} %stack.2), calls=%async_computation.1 | async-start | bytes 2097152 | tf_op jit(solution)/shard_map/all_to_all | solution.py:68
  235.4 31.9 %collective-permute-start.1 = (f32[1,1,8192]{2,1,0:T(1,128)S(1)}, f32[1,1,8192]{2,1,0:T(1,128)S(1)}, u32[]{:S(2)}, u32[]{:S(2)}) collective-permute-start(f32[1,1,8192]{2,1,0:T(1,128)S(1)} %get-tuple-element.7), channel_id=1, source_target_pairs={{1,0},{2,1},{3,2},{5,4},{6,5},{7,6},{9,8},{10,9},{11,10},{13,12},{... | collective-permute-start | bytes 98312 | tf_op jit(solution)/shard_map/ppermute | solution.py:23
  263.2 5.0 %collective-permute-start = (f32[1,1,8192]{2,1,0:T(1,128)S(1)}, f32[1,1,8192]{2,1,0:T(1,128)S(1)}, u32[]{:S(2)}, u32[]{:S(2)}) collective-permute-start(f32[1,1,8192]{2,1,0:T(1,128)S(1)} %get-tuple-element.6), channel_id=1, source_target_pairs={{0,1},{1,2},{2,3},{4,5},{5,6},{6,7},{8,9},{9,10},{10,11},{12,13},{... | collective-permute-start | bytes 98312 | tf_op jit(solution)/shard_map/ppermute | solution.py:21
  274.5 7.7 %collective-permute-start.3 = (f32[1,1,8192]{2,1,0:T(1,128)S(1)}, f32[1,1,8192]{2,1,0:T(1,128)S(1)}, u32[]{:S(2)}, u32[]{:S(2)}) collective-permute-start(f32[1,1,8192]{2,1,0:T(1,128)S(1)} %get-tuple-element.5), channel_id=1, source_target_pairs={{1,0},{2,1},{3,2},{5,4},{6,5},{7,6},{9,8},{10,9},{11,10},{13,12},{... | collective-permute-start | bytes 98312 | tf_op jit(solution)/shard_map/ppermute | solution.py:23
  276.5 6.7 %collective-permute-start.2 = (f32[1,1,8192]{2,1,0:T(1,128)S(1)}, f32[1,1,8192]{2,1,0:T(1,128)S(1)}, u32[]{:S(2)}, u32[]{:S(2)}) collective-permute-start(f32[1,1,8192]{2,1,0:T(1,128)S(1)} %get-tuple-element.4), channel_id=1, source_target_pairs={{0,1},{1,2},{2,3},{4,5},{5,6},{6,7},{8,9},{9,10},{10,11},{12,13},{... | collective-permute-start | bytes 98312 | tf_op jit(solution)/shard_map/ppermute | solution.py:21
Sparse Core Ops, SparseCore 0:
  55.2 144.9 reduce-scatter.1
